TPU v7x, 32 devices: a whole 2x2x4 slice. The times are simulated.
32 devices in a mesh: verts: 8 (over z, y), modes: 4 (over x, core).
Axes of the slice: x: 2, y: 2, z: 4, core: 2. Of those that a mesh axis runs over, the one named last changes fastest.
Arguments:
- reduced_coords: float32 [256], P('modes'), may hold values from -4 to 4
- mode_basis: bfloat16 [256, 3, 8192], P('modes', None, 'verts'), may hold values from -0.375 to 0.375
- rest_shape: float32 [3, 8192], P(None, 'verts'), may hold values from -6 to 6
- stiffness: float32 [8192], P('verts'), may hold values from 0.2 to 2
- send_slots: int32 [8, 8, 16], P('verts'), may hold values from 0 to 1023
- pair_peer: int32 [8, 2, 1024], P('verts'), may hold values from 0 to 7
- pair_slot: int32 [8, 2, 1024], P('verts'), may hold values from 0 to 15
- pair_count: int32 [8], P('verts'), may hold values from 1 to 1024, 4096 in all
Outputs:
- hessian: float32 [256, 256], P('modes')
- gradient: float32 [256], P('modes')
Inputs may be any that keep to these rules, and one draw needn't show every extreme that they name: `send_slots`: indices may repeat. `pair_count`: the counts sum to 8 * 512 and the busiest owner has all 1024 slots live; slots at and beyond an owner's count hold valid but unused indices.
All inputs are finite; a program needn't handle non-finite values. No bound on the sum of `pair_count` on one device may be relied on, other than what follows from the above.
Results may differ from a plain program's by a relative error of at most 0.0046.
Values may be sent and summed in bfloat16 or wider, within the bound.
No kernel may reach another device: no remote copies, remote signals or barrier semaphores. Data moves between devices by JAX's collectives and lax.ppermute only.
A program may use at most 64 MiB of HBM per device.

v0:
```python
import jax
import jax.numpy as jnp
from jax import lax
from jax.sharding import PartitionSpec as P

highest = lax.Precision.HIGHEST
barrier_reach = 1.5
gap_offset = 0.1


def barrier_slopes(distance):
    excess = distance - barrier_reach
    ratio_log = jnp.log(distance / barrier_reach)
    slope_term = -(2.0 * excess * ratio_log + excess * excess / distance)
    curvature = -(
        2.0 * ratio_log + 4.0 * excess / distance - excess * excess / (distance * distance)
    )
    inside = distance < barrier_reach
    return (jnp.where(inside, slope_term, 0.0), jnp.where(inside, curvature, 0.0))


def outer_sum(left_rows, right_rows):
    return lax.dot_general(
        left_rows, right_rows, (((1,), (1,)), ((), ())), preferred_element_type=jnp.float32
    )


def spring_terms(displacement, stiffness):
    radius = jnp.sqrt(1.0 + jnp.sum(displacement * displacement, axis=0))
    spring_rate = stiffness / radius
    return (spring_rate, -spring_rate / (radius * radius), spring_rate * displacement)


def elastic_left(basis_block, displacement, spring_rate, curvature_rate):
    mode_count, _, vertex_count = basis_block.shape
    projected = jnp.sum(basis_block * displacement[None], axis=1)
    scaled = (spring_rate * basis_block).astype(jnp.bfloat16)
    return jnp.concatenate(
        [
            scaled.reshape(mode_count, 3 * vertex_count),
            (curvature_rate * projected).astype(jnp.bfloat16),
        ],
        axis=1,
    )


def elastic_right(basis_block, displacement):
    mode_count, _, vertex_count = basis_block.shape
    projected = jnp.sum(basis_block * displacement[None], axis=1)
    return jnp.concatenate(
        [basis_block.reshape(mode_count, 3 * vertex_count), projected.astype(jnp.bfloat16)], axis=1
    )


def contact_terms(rows_first, rows_second, separation, active):
    mode_count, _, slot_total = rows_first.shape
    distance = jnp.sum(separation * separation, axis=0) + gap_offset
    slope_term, curvature = barrier_slopes(distance)
    slope_term = slope_term * active
    curvature = curvature * active
    difference = rows_first.astype(jnp.float32) - rows_second.astype(jnp.float32)
    leverage = jnp.sum(difference * separation[None], axis=1)
    left_rows = jnp.concatenate(
        [
            (2.0 * slope_term * difference)
            .astype(jnp.bfloat16)
            .reshape(mode_count, 3 * slot_total),
            (4.0 * curvature * leverage).astype(jnp.bfloat16),
        ],
        axis=1,
    )
    right_rows = jnp.concatenate(
        [
            difference.astype(jnp.bfloat16).reshape(mode_count, 3 * slot_total),
            leverage.astype(jnp.bfloat16),
        ],
        axis=1,
    )
    contact_grad = jnp.sum(difference * (2.0 * slope_term * separation)[None], axis=(1, 2))
    return (left_rows, right_rows, contact_grad)


def body(
    reduced_coords, mode_basis, rest_shape, stiffness, send_slots, pair_peer, pair_slot, pair_count
):
    local_modes, _, vertex_count = mode_basis.shape
    peer_count = lax.axis_size("verts")
    mode_groups = lax.axis_size("modes")
    mode_count = local_modes * mode_groups
    factor = mode_count / (3.0 * vertex_count * peer_count)
    partial_value = jnp.dot(
        reduced_coords,
        mode_basis.reshape(local_modes, 3 * vertex_count),
        precision=highest,
        preferred_element_type=jnp.float32,
    ).reshape(3, vertex_count)
    positions = rest_shape + lax.psum(partial_value, "modes")
    displacement = positions - rest_shape
    spring_rate, curvature_rate, elastic_force = spring_terms(displacement, stiffness)
    send_ids = send_slots[0]
    slot_count = send_ids.shape[1]
    flat_slots = send_ids.reshape(-1)
    outgoing_pos = jnp.take(positions, flat_slots, axis=1).reshape(3, peer_count, slot_count)
    outgoing_rows = jnp.take(mode_basis, flat_slots, axis=2).reshape(
        local_modes, 3, peer_count, slot_count
    )
    incoming_pos = lax.all_to_all(outgoing_pos, "verts", split_axis=1, concat_axis=1, tiled=True)
    incoming_rows = lax.all_to_all(outgoing_rows, "verts", split_axis=2, concat_axis=2, tiled=True)
    slot_total = pair_peer.shape[2]
    endpoints = (pair_peer[0] * slot_count + pair_slot[0]).reshape(-1)
    pos_ends = jnp.take(
        incoming_pos.reshape(3, peer_count * slot_count), endpoints, axis=1
    ).reshape(3, 2, slot_total)
    row_ends = jnp.take(
        incoming_rows.reshape(local_modes, 3, peer_count * slot_count), endpoints, axis=2
    ).reshape(local_modes, 3, 2, slot_total)
    separation = pos_ends[:, 0] - pos_ends[:, 1]
    active = (jnp.arange(slot_total, dtype=jnp.int32) < pair_count[0]).astype(jnp.float32)
    contact_left, contact_right, contact_grad = contact_terms(
        row_ends[:, :, 0], row_ends[:, :, 1], separation, active
    )
    left_rows = elastic_left(mode_basis, displacement, spring_rate, curvature_rate)
    hessian = outer_sum(
        left_rows,
        elastic_right(lax.all_gather(mode_basis, "modes", axis=0, tiled=True), displacement),
    )
    hessian = hessian + outer_sum(
        contact_left, lax.all_gather(contact_right, "modes", axis=0, tiled=True)
    )
    elastic_grad = jnp.dot(
        mode_basis.reshape(local_modes, 3 * vertex_count),
        elastic_force.reshape(3 * vertex_count),
        precision=highest,
        preferred_element_type=jnp.float32,
    )
    hessian, gradient = lax.psum((hessian, elastic_grad + contact_grad), "verts")
    return (hessian * factor, gradient * factor)


def solution(mesh):
    return jax.shard_map(
        body,
        mesh=mesh,
        in_specs=(
            P("modes"),
            P("modes", None, "verts"),
            P(None, "verts"),
            P("verts"),
            P("verts", None, None),
            P("verts", None, None),
            P("verts", None, None),
            P("verts"),
        ),
        out_specs=(P("modes", None), P("modes")),
        check_vma=False,
    )
```

profile of v0, /device:TPU:0, one launch (start us, length us, event | category | flops | bytes accessed | tf_op | source)
XLA Modules:
  0.0 166.1 jit_solution(15953994613902127670)
XLA Ops:
  7.9 0.8 reshape_squeeze.6
  9.4 1.3 fusion.20
  10.7 12.8 %psum.21 = f32[3,1024]{1,0:T(4,128)S(1)} all-reduce(f32[3,1024]{1,0:T(4,128)S(1)} %bitcast.91), channel_id=1, replica_groups=mesh['verts'=8,'modes'=4] {'modes'}, use_global_device_ids=true, to_apply=%region_0.0 | all-reduce | flops 3072 | bytes 24576 | tf_op jit(solution)/shard_map/psum | solution.py:97
  23.4 0.7 multiply_reduce_fusion.2
  25.8 5.9 %all-to-all-start = ((f32[3,8,16]{2,0,1:T(4,128)}), f32[3,8,16]{2,0,1:T(4,128)S(1)}, u32[]{:S(2)}, u32[]{:S(2)}) async-start(f32[3,8,16]{2,0,1:T(4,128)} %broadcast_select_fusion.3), calls=%async_computation | async-start | bytes 32768 | tf_op jit(solution)/shard_map/all_to_all | solution.py:107
  32.4 0.7 compare_and_fusion
  33.9 0.7 gather_fusion.2
  35.4 0.7 reshape.268
  36.2 2.1 %all-to-all-done = f32[3,8,16]{2,0,1:T(4,128)S(1)} async-done(((f32[3,8,16]{2,0,1:T(4,128)}), f32[3,8,16]{2,0,1:T(4,128)S(1)}, u32[]{:S(2)}, u32[]{:S(2)}) %all-to-all-start) | async-done | bytes 1568 | tf_op jit(solution)/shard_map/all_to_all | solution.py:107
  38.3 3.9 %all-to-all-start.1 = ((bf16[8,2,1536]{2,1,0:T(2,128)(2,1)}), bf16[8,2,1536]{2,1,0:T(2,128)(2,1)S(1)}, u32[]{:S(2)}, u32[]{:S(2)}) async-start(bf16[8,2,1536]{2,1,0:T(2,128)(2,1)} %reshape.268), calls=%async_computation.1 | async-start | bytes 98304 | tf_op jit(solution)/shard_map/all_to_all | solution.py:108
  42.4 5.5 %gather_fusion.1 = f32[2048,3]{1,0:T(8,128)S(1)} fusion(f32[3,128]{0,1:T(8,128)S(1)} %bitcast.82, s32[2048]{0:T(1024)S(1)} %broadcast_clamp_fusion), kind=kCustom, calls=%fused_computation.1 | custom fusion | bytes 57344 | tf_op jit(solution)/shard_map/jit(_take)/gather | solution.py:111
  48.2 0.7 all-to-all-done.1
  49.2 6.9 %gather_fusion.3 = bf16[2048,64,3]{1,2,0:T(4,128)(2,1)S(1)} fusion(bf16[64,3,128]{0,1,2:T(4,128)(2,1)S(1)} %copy.73, s32[2048]{0:T(1024)S(1)} %broadcast_clamp_fusion), kind=kCustom, calls=%fused_computation.3 | custom fusion | bytes 1581056 | tf_op jit(solution)/shard_map/jit(_take)/gather | solution.py:114
  56.1 1.6 copy.74
  59.0 1.4 fusion.9
  61.0 0.8 pad_maximum_fusion
  62.1 0.8 copy.80
  64.0 21.1 %psum.23 = f32[64]{0:T(128)S(1)} all-reduce(f32[64]{0:T(128)S(1)} %fusion.7), channel_id=1, replica_groups=mesh['verts'=8,'modes'=4] {'verts'}, use_global_device_ids=true, to_apply=%region_8.9 | all-reduce | flops 64 | bytes 512 | tf_op jit(solution)/shard_map/psum | solution.py:136
  85.2 1.9 %multiply_reduce_fusion = bf16[256,1024]{1,0:T(8,128)(2,1)S(1)} fusion(bf16[256,3,1024]{2,0,1:T(8,128)(2,1)} %all-gather.3.cloned.1.call-done, f32[3,1024]{1,0:T(4,128)} %copy-done.6), kind=kLoop, calls=%fused_computation.4 | loop fusion | flops 2097152 | bytes 2109440 | tf_op jit(solution)/shard_map/reduce_sum | solution.py:49
  87.1 1.0 copy.64
  88.8 2.5 %fusion.15 = f32[64,256]{1,0:T(8,128)S(1)} fusion(bf16[256,4096]{1,0:T(8,128)(2,1)} %all-gather.5.cloned.1.call-done, bf16[64,1024]{1,0:T(8,128)(2,1)} %get-tuple-element.11, bf16[64,3072]{1,0:T(8,128)(2,1)S(1)} %multiply_convert_fusion), kind=kOutput, calls=%fused_computation.26 | convolution fusion | flops 135266304 | bytes 2686976 | tf_op jit(solution)/shard_map/dot_general | solution.py:23
  91.4 1.1 fusion.4
  93.0 65.1 %all-reduce.2.cloned.1.call-done = f32[64,256]{1,0:T(8,128)} async-done(((f32[64,256]{1,0:T(8,128)}), f32[64,256]{1,0:T(8,128)}) %all-reduce.2.cloned.1.call-update) | async-done | bytes 65552 | tf_op jit(solution)/shard_map/psum | solution.py:136
  158.1 1.5 broadcast_multiply_fusion
  (65 shorter events, 10.0 us)
Async XLA Ops:
  7.2 2.2 %copy-start = (f32[64]{0:T(128)S(1)}, f32[64]{0:T(128)}, u32[]{:S(2)}) copy-start(f32[64]{0:T(128)} %param.8) | copy-start | bytes 772
  7.2 26.0 %copy-start.2 = (bf16[64,3,1024]{2,0,1:T(8,128)(2,1)S(1)}, bf16[64,3,1024]{2,0,1:T(8,128)(2,1)}, u32[]{:S(2)}) copy-start(bf16[64,3,1024]{2,0,1:T(8,128)(2,1)} %param.9) | copy-start | bytes 1179652
  7.2 78.0 %all-gather.3.cloned.1.call-start = ((), (), s32[]{:S(2)}) async-start(), calls=%async_computation.2 | async-start | bytes 1966080 | tf_op jit(solution)/shard_map/all_gather | solution.py:125
  24.2 38.7 %copy-start.6 = (f32[3,1024]{1,0:T(4,128)}, f32[3,1024]{1,0:T(4,128)S(1)}, u32[]{:S(2)}) copy-start(f32[3,1024]{1,0:T(4,128)S(1)} %get-tuple-element.5) | copy-start | bytes 36868
  25.8 12.5 %all-to-all-start = ((f32[3,8,16]{2,0,1:T(4,128)}), f32[3,8,16]{2,0,1:T(4,128)S(1)}, u32[]{:S(2)}, u32[]{:S(2)}) async-start(f32[3,8,16]{2,0,1:T(4,128)} %broadcast_select_fusion.3), calls=%async_computation | async-start | bytes 32768 | tf_op jit(solution)/shard_map/all_to_all | solution.py:107
  38.3 10.7 %all-to-all-start.1 = ((bf16[8,2,1536]{2,1,0:T(2,128)(2,1)}), bf16[8,2,1536]{2,1,0:T(2,128)(2,1)S(1)}, u32[]{:S(2)}, u32[]{:S(2)}) async-start(bf16[8,2,1536]{2,1,0:T(2,128)(2,1)} %reshape.268), calls=%async_computation.1 | async-start | bytes 98304 | tf_op jit(solution)/shard_map/all_to_all | solution.py:108
  42.2 46.6 %all-gather.5.cloned.1.call-start = ((), (), s32[]{:S(2)}) async-start(), calls=%async_computation.3 | async-start | bytes 2621440 | tf_op jit(solution)/shard_map/all_gather | solution.py:128
  58.9 3.1 %copy-start.8 = (f32[1024]{0:T(1024)S(1)}, f32[1024]{0:T(1024)}, u32[]{:S(2)}) copy-start(f32[1024]{0:T(1024)} %param.11) | copy-start | bytes 12292
  58.9 3.1 %copy-start.3 = (bf16[64,3,1024]{2,0,1:T(8,128)(2,1)S(1)}, bf16[64,3,1024]{2,0,1:T(8,128)(2,1)}, u32[]{:S(2)}) copy-start(bf16[64,3,1024]{2,0,1:T(8,128)(2,1)} %param.9) | copy-start | bytes 1179652
  61.9 96.2 %all-reduce.2.cloned.1.call-start = ((), (), s32[]{:S(2)}) async-start(), calls=%async_computation.4 | async-start | bytes 131072 | tf_op jit(solution)/shard_map/psum | solution.py:136
  85.2 2.9 %copy-start.1 = (bf16[256,3,1024]{2,0,1:T(8,128)(2,1)S(1)}, bf16[256,3,1024]{2,0,1:T(8,128)(2,1)}, u32[]{:S(2)}) copy-start(bf16[256,3,1024]{2,0,1:T(8,128)(2,1)} %all-gather.3.cloned.1.call-done) | copy-start | bytes 4718596
  88.8 2.6 %copy-start.4 = (bf16[256,1024]{0,1:T(8,128)(2,1)S(1)}, bf16[256,1024]{0,1:T(8,128)(2,1)}, u32[]{:S(2)}) copy-start(bf16[256,1024]{0,1:T(8,128)(2,1)} %copy.64) | copy-start | bytes 1572868
  88.8 2.6 %copy-start.5 = (bf16[3,8,8,1024]{3,2,0,1:T(8,128)(2,1)S(1)}, bf16[3,8,8,1024]{3,2,0,1:T(8,128)(2,1)}, u32[]{:S(2)}) copy-start(bf16[3,8,8,1024]{3,2,0,1:T(8,128)(2,1)} %copy.80) | copy-start | bytes 1179652
  88.8 2.6 %copy-start.7 = (bf16[64,1024]{1,0:T(8,128)(2,1)S(1)}, bf16[64,1024]{1,0:T(8,128)(2,1)}, u32[]{:S(2)}) copy-start(bf16[64,1024]{1,0:T(8,128)(2,1)} %multiply_convert_fusion.2) | copy-start | bytes 393220
Sparse Core Ops, SparseCore 0:
  9.6 22.3 all-gather.2
  62.0 22.2 all-gather.4
  92.6 65.4 all-reduce.1
where the time goes:
time: 167 us; the launch traced here: 166 us
  waiting for transfers between devices  68.7 us (41%)
  blocking collectives  33.8 us (20%)
  local copies, waits for them, and re-layouts  21.5 us (13%)
  between operations  14.8 us (9%)
  other arithmetic  12.1 us (7%)
  starting transfers between devices  9.92 us (6%)
  matrix products  5.31 us (3%)
    psum x1, waiting for transfers between devices, body(): lax.psum((hessian, elastic_grad + contact_grad), 'verts')  65.1 us
    psum x1, blocking collectives, body(): lax.psum((hessian, elastic_grad + contact_grad), 'verts')  21.1 us
    psum x1, blocking collectives, body(): positions = rest_shape + lax.psum(partial_value, 'modes')  12.8 us
    gather x2, local copies, waits for them, and re-layouts, body(): jnp.take(incoming_rows.reshape(local_modes, 3, peer_count * slot_count),...  8.42 us
    all_to_all x1, starting transfers between devices, body(): lax.all_to_all(outgoing_pos, 'verts', split_axis=1, concat_axis=1, tiled=...  5.89 us
    gather x2, local copies, waits for them, and re-layouts, body(): jnp.take(incoming_pos.reshape(3, peer_count * slot_count), endpoints, axi...  5.79 us
    all_to_all x1, starting transfers between devices, body(): lax.all_to_all(outgoing_rows, 'verts', split_axis=2, concat_axis=2, tiled...  3.92 us
    dot_general x2, matrix products, outer_sum(): lax.dot_general(left_rows, right_rows, (((1,), (1,)), ((), ())), preferre...  3.62 us
  transfers between devices with their start and end apart: 5, of which 3 were waited for; matrix products, arithmetic and copies ran while one was open for 20% of the time, Pallas kernels for 0%

commit v1 on v0

--- a/solution.py
+++ b/solution.py
@@ -2,6 +2,7 @@
 import jax.numpy as jnp
 from jax import lax
 from jax.sharding import PartitionSpec as P
+from jax.lax import all_gather
 
 highest = lax.Precision.HIGHEST
 barrier_reach = 1.5
@@ -94,7 +95,8 @@
         precision=highest,
         preferred_element_type=jnp.float32,
     ).reshape(3, vertex_count)
-    positions = rest_shape + lax.psum(partial_value, "modes")
+    _handle_edge = lambda u: jnp.sum(all_gather(u, "modes"), 0)
+    positions = rest_shape + _handle_edge(partial_value)
     displacement = positions - rest_shape
     spring_rate, curvature_rate, elastic_force = spring_terms(displacement, stiffness)
     send_ids = send_slots[0]

time: 167 us -> 162 us (0.970)
  blocking collectives: 33.8 us -> 27.3 us
    psum x1 -> x0, blocking collectives: 12.8 us -> none  [body(): positions = rest_shape + lax.psum(partial_value, 'modes')]
    all_gather x0 -> x1, blocking collectives: none -> 6.18 us  [body(): _handle_edge = lambda u: jnp.sum(all_gather(u, 'modes'), 0)]
  transfers between devices with their start and end apart: 5 -> 5, of which waited for: 3 -> 3; matrix products, arithmetic and copies ran while one was open for 20% -> 21% of each run, Pallas kernels for 0% -> 0%
where the time goes in v1:
time: 162 us; the launch traced here: 161 us
  waiting for transfers between devices  69.7 us (43%)
  blocking collectives  27.3 us (17%)
  local copies, waits for them, and re-layouts  21.5 us (13%)
  between operations  14.8 us (9%)
  other arithmetic  12.1 us (7%)
  starting transfers between devices  10.4 us (6%)
  matrix products  5.31 us (3%)
    psum x1, waiting for transfers between devices, body(): lax.psum((hessian, elastic_grad + contact_grad), 'verts')  66.1 us
    psum x1, blocking collectives, body(): lax.psum((hessian, elastic_grad + contact_grad), 'verts')  21.1 us
    gather x2, local copies, waits for them, and re-layouts, body(): jnp.take(incoming_rows.reshape(local_modes, 3, peer_count * slot_count),...  8.42 us
    all_to_all x1, starting transfers between devices, body(): lax.all_to_all(outgoing_pos, 'verts', split_axis=1, concat_axis=1, tiled=...  6.36 us
    all_gather x1, blocking collectives, body(): _handle_edge = lambda u: jnp.sum(all_gather(u, 'modes'), 0)  6.18 us
    gather x2, local copies, waits for them, and re-layouts, body(): jnp.take(incoming_pos.reshape(3, peer_count * slot_count), endpoints, axi...  5.79 us
    all_to_all x1, starting transfers between devices, body(): lax.all_to_all(outgoing_rows, 'verts', split_axis=2, concat_axis=2, tiled...  3.92 us
    dot_general x2, matrix products, outer_sum(): lax.dot_general(left_rows, right_rows, (((1,), (1,)), ((), ())), preferre...  3.61 us
  transfers between devices with their start and end apart: 5, of which 3 were waited for; matrix products, arithmetic and copies ran while one was open for 21% of the time, Pallas kernels for 0%

profile of v1, /device:TPU:0, one launch (start us, length us, event | category | flops | bytes accessed | tf_op | source)
XLA Modules:
  0.0 161.1 jit_solution(10486775143674730210)
XLA Ops:
  7.9 0.8 reshape_squeeze.6
  9.4 1.3 fusion.20
  10.7 6.2 %all-gather.1 = f32[4,3,1024]{2,1,0:T(4,128)S(1)} all-gather(f32[1,3,1024]{2,1,0:T(4,128)S(1)} %copy.77), channel_id=2, replica_groups=mesh['verts'=8,'modes'=4] {'modes'}, dimensions={0}, use_global_device_ids=true | all-gather | bytes 61440 | tf_op jit(solution)/shard_map/all_gather | solution.py:98
  16.9 0.7 multiply_reduce_fusion.2
  19.3 6.4 %all-to-all-start = ((f32[3,8,16]{2,0,1:T(4,128)}), f32[3,8,16]{2,0,1:T(4,128)S(1)}, u32[]{:S(2)}, u32[]{:S(2)}) async-start(f32[3,8,16]{2,0,1:T(4,128)} %broadcast_select_fusion.3), calls=%async_computation | async-start | bytes 32768 | tf_op jit(solution)/shard_map/all_to_all | solution.py:109
  26.3 0.7 compare_and_fusion
  27.8 0.7 gather_fusion.2
  29.4 0.7 reshape.277
  30.1 2.1 %all-to-all-done = f32[3,8,16]{2,0,1:T(4,128)S(1)} async-done(((f32[3,8,16]{2,0,1:T(4,128)}), f32[3,8,16]{2,0,1:T(4,128)S(1)}, u32[]{:S(2)}, u32[]{:S(2)}) %all-to-all-start) | async-done | bytes 1568 | tf_op jit(solution)/shard_map/all_to_all | solution.py:109
  32.2 3.9 %all-to-all-start.1 = ((bf16[8,2,1536]{2,1,0:T(2,128)(2,1)}), bf16[8,2,1536]{2,1,0:T(2,128)(2,1)S(1)}, u32[]{:S(2)}, u32[]{:S(2)}) async-start(bf16[8,2,1536]{2,1,0:T(2,128)(2,1)} %reshape.277), calls=%async_computation.1 | async-start | bytes 98304 | tf_op jit(solution)/shard_map/all_to_all | solution.py:110
  36.3 5.5 %gather_fusion.1 = f32[2048,3]{1,0:T(8,128)S(1)} fusion(f32[3,128]{0,1:T(8,128)S(1)} %bitcast.80, s32[2048]{0:T(1024)S(1)} %broadcast_clamp_fusion), kind=kCustom, calls=%fused_computation.1 | custom fusion | bytes 57344 | tf_op jit(solution)/shard_map/jit(_take)/gather | solution.py:113
  42.2 0.7 all-to-all-done.1
  43.1 6.9 %gather_fusion.3 = bf16[2048,64,3]{1,2,0:T(4,128)(2,1)S(1)} fusion(bf16[64,3,128]{0,1,2:T(4,128)(2,1)S(1)} %copy.74, s32[2048]{0:T(1024)S(1)} %broadcast_clamp_fusion), kind=kCustom, calls=%fused_computation.3 | custom fusion | bytes 1581056 | tf_op jit(solution)/shard_map/jit(_take)/gather | solution.py:116
  50.0 1.6 copy.75
  52.9 1.4 fusion.9
  55.0 0.8 pad_maximum_fusion
  56.0 0.8 copy.81
  58.0 21.1 %psum.15 = f32[64]{0:T(128)S(1)} all-reduce(f32[64]{0:T(128)S(1)} %fusion.7), channel_id=1, replica_groups=mesh['verts'=8,'modes'=4] {'verts'}, use_global_device_ids=true, to_apply=%region_8.9 | all-reduce | flops 64 | bytes 512 | tf_op jit(solution)/shard_map/psum | solution.py:138
  79.1 1.9 %multiply_reduce_fusion = bf16[256,1024]{1,0:T(8,128)(2,1)S(1)} fusion(bf16[256,3,1024]{2,0,1:T(8,128)(2,1)} %all-gather.5.cloned.1.call-done, f32[3,1024]{1,0:T(4,128)} %copy-done.6), kind=kLoop, calls=%fused_computation.4 | loop fusion | flops 2097152 | bytes 2109440 | tf_op jit(solution)/shard_map/reduce_sum | solution.py:50
  81.0 1.0 copy.65
  82.7 2.5 %fusion.15 = f32[64,256]{1,0:T(8,128)S(1)} fusion(bf16[256,4096]{1,0:T(8,128)(2,1)} %all-gather.7.cloned.1.call-done, bf16[64,1024]{1,0:T(8,128)(2,1)} %get-tuple-element.11, bf16[64,3072]{1,0:T(8,128)(2,1)S(1)} %multiply_convert_fusion), kind=kOutput, calls=%fused_computation.26 | convolution fusion | flops 135266304 | bytes 2686976 | tf_op jit(solution)/shard_map/dot_general | solution.py:24
  85.3 1.1 fusion.4
  86.9 66.1 %all-reduce.2.cloned.1.call-done = f32[64,256]{1,0:T(8,128)} async-done(((f32[64,256]{1,0:T(8,128)}), f32[64,256]{1,0:T(8,128)}) %all-reduce.2.cloned.1.call-update) | async-done | bytes 65552 | tf_op jit(solution)/shard_map/psum | solution.py:138
  153.1 1.5 broadcast_multiply_fusion
  (66 shorter events, 10.0 us)
Async XLA Ops:
  7.2 2.2 %copy-start = (f32[64]{0:T(128)S(1)}, f32[64]{0:T(128)}, u32[]{:S(2)}) copy-start(f32[64]{0:T(128)} %param.8) | copy-start | bytes 772
  7.2 19.9 %copy-start.2 = (bf16[64,3,1024]{2,0,1:T(8,128)(2,1)S(1)}, bf16[64,3,1024]{2,0,1:T(8,128)(2,1)}, u32[]{:S(2)}) copy-start(bf16[64,3,1024]{2,0,1:T(8,128)(2,1)} %param.9) | copy-start | bytes 1179652
  7.2 71.9 %all-gather.5.cloned.1.call-start = ((), (), s32[]{:S(2)}) async-start(), calls=%async_computation.2 | async-start | bytes 1966080 | tf_op jit(solution)/shard_map/all_gather | solution.py:127
  17.6 39.2 %copy-start.6 = (f32[3,1024]{1,0:T(4,128)}, f32[3,1024]{1,0:T(4,128)S(1)}, u32[]{:S(2)}) copy-start(f32[3,1024]{1,0:T(4,128)S(1)} %get-tuple-element.5) | copy-start | bytes 36868
  19.3 12.9 %all-to-all-start = ((f32[3,8,16]{2,0,1:T(4,128)}), f32[3,8,16]{2,0,1:T(4,128)S(1)}, u32[]{:S(2)}, u32[]{:S(2)}) async-start(f32[3,8,16]{2,0,1:T(4,128)} %broadcast_select_fusion.3), calls=%async_computation | async-start | bytes 32768 | tf_op jit(solution)/shard_map/all_to_all | solution.py:109
  32.2 10.7 %all-to-all-start.1 = ((bf16[8,2,1536]{2,1,0:T(2,128)(2,1)}), bf16[8,2,1536]{2,1,0:T(2,128)(2,1)S(1)}, u32[]{:S(2)}, u32[]{:S(2)}) async-start(bf16[8,2,1536]{2,1,0:T(2,128)(2,1)} %reshape.277), calls=%async_computation.1 | async-start | bytes 98304 | tf_op jit(solution)/shard_map/all_to_all | solution.py:110
  36.1 46.6 %all-gather.7.cloned.1.call-start = ((), (), s32[]{:S(2)}) async-start(), calls=%async_computation.3 | async-start | bytes 2621440 | tf_op jit(solution)/shard_map/all_gather | solution.py:130
  52.8 3.1 %copy-start.8 = (f32[1024]{0:T(1024)S(1)}, f32[1024]{0:T(1024)}, u32[]{:S(2)}) copy-start(f32[1024]{0:T(1024)} %param.11) | copy-start | bytes 12292
  52.8 3.1 %copy-start.3 = (bf16[64,3,1024]{2,0,1:T(8,128)(2,1)S(1)}, bf16[64,3,1024]{2,0,1:T(8,128)(2,1)}, u32[]{:S(2)}) copy-start(bf16[64,3,1024]{2,0,1:T(8,128)(2,1)} %param.9) | copy-start | bytes 1179652
  55.8 97.2 %all-reduce.2.cloned.1.call-start = ((), (), s32[]{:S(2)}) async-start(), calls=%async_computation.4 | async-start | bytes 131072 | tf_op jit(solution)/shard_map/psum | solution.py:138
  79.1 2.9 %copy-start.1 = (bf16[256,3,1024]{2,0,1:T(8,128)(2,1)S(1)}, bf16[256,3,1024]{2,0,1:T(8,128)(2,1)}, u32[]{:S(2)}) copy-start(bf16[256,3,1024]{2,0,1:T(8,128)(2,1)} %all-gather.5.cloned.1.call-done) | copy-start | bytes 4718596
  82.7 2.6 %copy-start.4 = (bf16[256,1024]{0,1:T(8,128)(2,1)S(1)}, bf16[256,1024]{0,1:T(8,128)(2,1)}, u32[]{:S(2)}) copy-start(bf16[256,1024]{0,1:T(8,128)(2,1)} %copy.65) | copy-start | bytes 1572868
  82.7 2.6 %copy-start.5 = (bf16[3,8,8,1024]{3,2,0,1:T(8,128)(2,1)S(1)}, bf16[3,8,8,1024]{3,2,0,1:T(8,128)(2,1)}, u32[]{:S(2)}) copy-start(bf16[3,8,8,1024]{3,2,0,1:T(8,128)(2,1)} %copy.81) | copy-start | bytes 1179652
  82.7 2.6 %copy-start.7 = (bf16[64,1024]{1,0:T(8,128)(2,1)S(1)}, bf16[64,1024]{1,0:T(8,128)(2,1)}, u32[]{:S(2)}) copy-start(bf16[64,1024]{1,0:T(8,128)(2,1)} %multiply_convert_fusion.2) | copy-start | bytes 393220
Sparse Core Ops, SparseCore 0:
  9.6 22.3 all-gather.4
  55.9 23.1 all-gather.6
  86.5 66.4 all-reduce.1
